TPU v7x, 32 devices: a whole 2x2x4 slice. The times are simulated.
32 devices in a mesh: tm: 4 (over z), tmpl: 8 (over y, x, core).
Axes of the slice: x: 2, y: 2, z: 4, core: 2. Of those that a mesh axis runs over, the one named last changes fastest.
Arguments:
- strain: float32 [8, 131072], P('tmpl', 'tm'), may hold values from -6 to 6
- psd_bins: int32 [4, 65536], P(None, 'tmpl'), may hold values from 0 to 8191, as said below
- psd_values: float32 [4, 8192], P('tm'), may hold values from 0.25 to 4
- chirp_slope: int32 [16], P('tmpl'), may hold values from 0 to 1023
- chirp_curve: int32 [16], P('tmpl'), may hold values from 1 to 63
Outputs:
- snr: float32 [16, 1048576], P('tmpl', 'tm')
Inputs may be any that keep to these rules, and one draw needn't show every extreme that they name: psd_bins[r, c] names the row of psd_values that serves frequency bin r * 65536 + c.
All inputs are finite; a program needn't handle non-finite values.
Results may differ from a plain program's by a relative error of at most 0.0003.
Values sent between devices are 32-bit elements; how exact they have to be, the bound alone decides.
A program may use at most 128 MiB of HBM per device.

v0:
```python
import functools
import math

import jax
import jax.numpy as jnp
import numpy as np
from jax import lax
from jax.experimental import pallas as pl
from jax.experimental.pallas import tpu as pltpu
from jax.sharding import PartitionSpec as P

TWO_PI = 2.0 * math.pi
LANE = 128
FINE = 32
COARSE = 16
VMEM_LIMIT = 60 * 1024 * 1024
BF16 = jnp.bfloat16
F32 = jnp.float32
NN = (((1,), (0,)), ((), ()))
NT = (((1,), (1,)), ((), ()))


def shifted(block, axis, distance):
    devices = range(lax.axis_size(axis))
    route = [(i - distance, i) for i in devices if i - distance in devices]
    return lax.ppermute(block, axis, route)


def base_table(rows, cols, modulus, direction, start=0):
    first = start + FINE * np.arange(rows // FINE, dtype=np.int64)
    index = np.concatenate([first, np.arange(FINE, dtype=np.int64)])
    angle = (index[:, None] * np.asarray(cols, dtype=np.int64)[None, :] % modulus) * (
        direction * TWO_PI / modulus
    )
    return jnp.asarray(np.stack([np.cos(angle), np.sin(angle)]).astype(np.float32))


def product_rows(table, outer, coarse_count):
    c1 = table[0, pl.ds(outer, 1), :]
    s1 = table[1, pl.ds(outer, 1), :]
    c0 = table[0, coarse_count : coarse_count + FINE, :]
    s0 = table[1, coarse_count : coarse_count + FINE, :]
    return c1 * c0 - s1 * s0, s1 * c0 + c1 * s0


def halves(value):
    high = value.astype(BF16)
    return high, (value - high.astype(F32)).astype(BF16)


def put(ref, slot, index, value):
    high, low = halves(value)
    ref[(slot, 0) + index] = high
    ref[(slot, 1) + index] = low


def put_factor(ref, index, re, im):
    put(ref, 0, index, re)
    put(ref, 1, index, im - re)
    put(ref, 2, index, re + im)


def split_dot(a_high, a_low, b_high, b_low, dims):
    ((a_axis,), (b_axis,)), _ = dims
    a = jnp.concatenate([a_high, a_low, a_high], axis=a_axis)
    b = jnp.concatenate([b_low, b_high, b_high], axis=b_axis)
    return lax.dot_general(a, b, dims, preferred_element_type=F32)


def dot3(a, b, slot, dims):
    return split_dot(a[slot, 0], a[slot, 1], b[slot, 0], b[slot, 1], dims)


def complex_dot(a, b, dims):
    k1 = dot3(a, b, 0, dims)
    k2 = dot3(a, b, 1, dims)
    k3 = dot3(a, b, 2, dims)
    return k1 - k3, k1 + k2


def look_up(bins, table_ref):
    high = bins // LANE
    low = bins % LANE

    def body(row, total):
        lanes = pl.ds(pl.multiple_of(row * LANE, LANE), LANE)
        line = jnp.broadcast_to(table_ref[:, lanes], bins.shape)
        return jnp.where(
            high == row,
            jnp.take_along_axis(line, low, axis=1, mode="promise_in_bounds"),
            total,
        )

    picked = lax.fori_loop(
        0, table_ref.shape[1] // LANE, body, jnp.ones(bins.shape, F32), unroll=4
    )
    return 1.0 / picked


def density_rows(bins_ref, ordered_ref, bands, inner):
    member_rows = bins_ref.shape[1] // inner
    for q in range(inner // LANE):
        for band in range(bands):
            for row in range(member_rows):
                start = row * inner + q * LANE
                target = (q * bands + band) * member_rows + row
                ordered_ref[target : target + 1, :] = bins_ref[
                    band : band + 1, start : start + LANE
                ]


def density_kernel(bands, inner, bins_ref, table_ref, out_ref, ordered_ref):
    density_rows(bins_ref, ordered_ref, bands, inner)
    out_ref[...] = look_up(ordered_ref[...], table_ref)


def amplitude_rows(first, shape, total_len):
    k_low = total_len // 200
    k_cut = 3 * total_len // 8
    row = first + lax.broadcasted_iota(jnp.int32, shape, 0)
    frequency = row * shape[1] + lax.broadcasted_iota(jnp.int32, shape, 1)
    ratio = jnp.maximum(frequency.astype(F32) / k_low, 1.0)
    inside = (frequency >= k_low) & (frequency < k_cut)
    return jnp.where(inside, jnp.exp(jnp.log(ratio) * (-7.0 / 6.0)), 0.0)


def template_rows(slope_ref, curve_ref, chirp_ref, m, total_len):
    inner = chirp_ref.shape[3]
    coarse = chirp_ref.shape[2] - COARSE
    for first in range(0, coarse + COARSE, 8):
        slope = slope_ref[m]
        curve = curve_ref[m]
        if first < coarse:
            row = first
            jump = COARSE * inner
        else:
            row = first - coarse
            jump = 0
        shape = (8, inner)
        index = row + lax.broadcasted_iota(jnp.int32, shape, 0)
        column = lax.broadcasted_iota(jnp.int32, shape, 1)
        mask = total_len - 1
        if jump:
            far = jump * index
            phase = slope * far + curve * ((2 * far * column) & mask)
        else:
            near = inner * index + column
            phase = slope * near + curve * ((near * near) & mask)
        angle = (phase & mask).astype(F32) * (TWO_PI / total_len)
        chirp_ref[m, 0, first : first + 8, :] = jnp.cos(angle)
        chirp_ref[m, 1, first : first + 8, :] = jnp.sin(angle)


def amplitude_table(amp_ref, total_len):
    depth, inner = amp_ref.shape

    @pl.loop(0, depth // 8)
    def _(i):
        first = pl.multiple_of(i * 8, 8)
        amp_ref[pl.ds(first, 8), :] = amplitude_rows(first, (8, inner), total_len)


def table_kernel(total_len, slope_ref, curve_ref, chirp_ref, amp_ref):
    for m in range(chirp_ref.shape[0]):
        template_rows(slope_ref, curve_ref, chirp_ref, m, total_len)
    amplitude_table(amp_ref, total_len)


def gather_kernel(
    bands, inner, total_len,
    own_ref, bins_ref, table_ref, slope_ref, curve_ref,
    out_ref, chirp_ref, amp_ref,
    ordered_ref, send_sem, recv_sem, tail_send, tail_recv,
):
    tm = lax.axis_index("tm")
    me = lax.axis_index("tmpl")
    count = lax.axis_size("tm")
    half = own_ref.shape[0]
    extra = ordered_ref.shape[0]

    def peer(distance):
        low = me % (2 * distance)
        return me - low + (low + distance) % (2 * distance)

    core = peer(1)
    side = peer(2)
    front = peer(4)
    side_front = side + front - me
    spans = ((half, half), (0, half), (2 * half, extra))

    barrier = pltpu.get_barrier_semaphore()
    for other in (core, side, front):
        pl.semaphore_signal(
            barrier, inc=1, device_id={"tmpl": other}, device_id_type=pl.DeviceIdType.MESH
        )

    for other in ((tm + 1) % count, (tm + count - 1) % count):
        pl.semaphore_signal(
            barrier, inc=1, device_id={"tm": other}, device_id_type=pl.DeviceIdType.MESH
        )
    pl.semaphore_wait(barrier, 5)

    def copy(part, kind, slot, piece, target, source=None):
        first, rows = spans[part]
        if part == 1 and kind in (1, 2):
            piece = 2 - kind
        if piece is not None:
            rows = rows // 2
            first = first + piece * rows
        view = out_ref.at[slot, pl.ds(first, rows), :]
        return pltpu.make_async_remote_copy(
            src_ref=view if source is None else source,
            dst_ref=view,
            send_sem=send_sem.at[part, kind],
            recv_sem=recv_sem.at[part, kind],
            device_id={"tmpl": target},
            device_id_type=pl.DeviceIdType.MESH,
        )

    def send(part, kind, source=None):
        slot, piece, target = (
            (me, None, core), (me, None, side), (me, None, front),
            (side, None, core), (front, None, core),
            (side, 0, front), (front, 1, side),
            (side_front, 0, core), (side_front, 1, core),
        )[kind]
        return copy(part, kind, slot, piece, target, source if kind < 3 else None)

    def first_stage(part, source=None):
        send(part, 1, source).start()
        send(part, 2, source).start()
        send(part, 0, source).start()

    def second_stage(part):
        copy(part, 1, side, None, side).wait_recv()
        send(part, 5).start()
        copy(part, 2, front, None, front).wait_recv()
        send(part, 6).start()
        send(part, 3).start()
        send(part, 4).start()

    def third_stage(part):
        copy(part, 5, side_front, 0, front).wait_recv()
        send(part, 7).start()
        copy(part, 6, side_front, 1, side).wait_recv()
        send(part, 8).start()

    def last_stage(part, source=None):
        other = core + side - me
        across = core + front - me
        corner = core + side_front - me
        copy(part, 0, core, None, core).wait_recv()
        copy(part, 3, other, None, core).wait_recv()
        copy(part, 4, across, None, core).wait_recv()
        copy(part, 7, corner, 0, core).wait_recv()
        copy(part, 8, corner, 1, core).wait_recv()
        for kind in range(9):
            if part != 1 or kind not in (5, 6):
                send(part, kind, source).wait_send()

    def onward(kind):
        slot, piece = ((me, None), (side, 0), (front, 1), (side_front, 0), (side_front, 1))[kind]
        rows = half if piece is None else half // 2
        first = 0 if piece is None else piece * rows
        source = own_ref if kind == 0 else out_ref.at[slot, pl.ds(half + first, rows), :]
        return pltpu.make_async_remote_copy(
            src_ref=source,
            dst_ref=out_ref.at[slot, pl.ds(first, rows), :],
            send_sem=tail_send.at[kind],
            recv_sem=tail_recv.at[kind],
            device_id={"tm": (tm + 1) % count},
            device_id_type=pl.DeviceIdType.MESH,
        )

    def pass_on(kinds):
        @pl.when(tm < count - 1)
        def _():
            for kind in kinds:
                onward(kind).start()

    def second_stage_old():
        copy(1, 1, side, None, side).wait_recv()
        onward(1).wait_recv()
        send(1, 3).start()
        copy(1, 2, front, None, front).wait_recv()
        onward(2).wait_recv()
        send(1, 4).start()

    def third_stage_old():
        onward(3).wait_recv()
        send(1, 7).start()
        onward(4).wait_recv()
        send(1, 8).start()

    pass_on((0,))
    first_stage(0, own_ref)
    out_ref[me, half : 2 * half, :] = own_ref[...]
    density_rows(bins_ref, ordered_ref, bands, inner)
    third = extra // 3

    def densities(i):
        rows = slice(i * third, (i + 1) * third)
        out_ref[me, 2 * half + i * third : 2 * half + (i + 1) * third, :] = look_up(
            ordered_ref[rows, :], table_ref
        )

    @pl.when(tm == 0)
    def _():
        for slot in range(out_ref.shape[0]):
            out_ref[slot, :half, :] = jnp.zeros((half, LANE), F32)

    @pl.when(tm > 0)
    def _():
        onward(0).wait_recv()
        first_stage(1)

    densities(0)
    second_stage(0)
    pass_on((1, 2))
    densities(1)
    third_stage(0)
    pass_on((3, 4))
    densities(2)
    first_stage(2)

    @pl.when(tm > 0)
    def _():
        second_stage_old()

    template_rows(slope_ref, curve_ref, chirp_ref, 0, total_len)
    second_stage(2)

    @pl.when(tm > 0)
    def _():
        third_stage_old()

    for m in range(1, chirp_ref.shape[0]):
        template_rows(slope_ref, curve_ref, chirp_ref, m, total_len)
    third_stage(2)
    amplitude_table(amp_ref, total_len)
    last_stage(0, own_ref)

    @pl.when(tm > 0)
    def _():
        last_stage(1)

    last_stage(2)

    @pl.when(tm < count - 1)
    def _():
        for kind in range(5):
            onward(kind).wait_send()


def forward_kernel(
    block, segment_rows, member_rows, templates, scale,
    packed_ref, f1_ref, twist_ref, f2_ref, amp_ref, chirp_ref,
    re_ref, im_ref, sigma_ref,
    x_ref, f1_buf, y_buf, f2_buf, weight_ref,
):
    step = pl.program_id(0)
    groups = packed_ref.shape[0]
    depth = re_ref.shape[1]
    coarse2 = depth // FINE
    f1_coarse = f1_ref.shape[1] - FINE
    twist_coarse = twist_ref.shape[1] - FINE

    @pl.when(step == 0)
    def _():
        for j in range(groups):
            high, low = halves(packed_ref[j, :segment_rows, :])
            x_ref[0, :, j * LANE : (j + 1) * LANE] = high
            x_ref[1, :, j * LANE : (j + 1) * LANE] = low

        @pl.loop(0, coarse2)
        def _(outer):
            c, s = product_rows(f2_ref, outer, coarse2)
            put_factor(f2_buf, (pl.ds(pl.multiple_of(outer * FINE, FINE), FINE),), c, s)

        sigma_ref[...] = jnp.zeros_like(sigma_ref)

    per_block = block // FINE

    @pl.loop(0, per_block)
    def _(i):
        rows = (pl.ds(pl.multiple_of(i * FINE, FINE), FINE),)
        c, s = product_rows(f1_ref, step * per_block + i, f1_coarse)
        put(f1_buf, 0, rows, c)
        put(f1_buf, 1, rows, s)

    def real_dot(slot):
        return split_dot(f1_buf[slot, 0], f1_buf[slot, 1], x_ref[0], x_ref[1], NN)

    y_re = real_dot(0)
    y_im = real_dot(1)
    for i in range(per_block):
        span = slice(i * FINE, (i + 1) * FINE)
        c, s = product_rows(twist_ref, step * per_block + i, twist_coarse)
        a, b = y_re[span], y_im[span]
        re = a * c - b * s
        im = a * s + b * c
        put(y_buf, 0, (span,), re + im)
        put(y_buf, 1, (span,), re)
        put(y_buf, 2, (span,), im)
    x_re, x_im = complex_dot(f2_buf, y_buf, NT)

    bands = (packed_ref.shape[1] - segment_rows) // member_rows // (re_ref.shape[2] * 2 // LANE)
    quarters = block // LANE
    all_quarters = (packed_ref.shape[1] - segment_rows) // (member_rows * bands)
    for q in range(quarters):
        lanes = slice(q * LANE, (q + 1) * LANE)
        for band in range(bands):
            for j in range(groups):
                source = segment_rows + ((step * quarters + q) * bands + band) * member_rows
                target = (band * groups + j) * member_rows
                weight_ref[target : target + member_rows, lanes] = packed_ref[
                    j, pl.ds(pl.multiple_of(source, 8), member_rows), :
                ]
    amp = amp_ref[...]
    weight = amp * weight_ref[...]
    sigma_ref[...] += jnp.sum((weight * amp).reshape(-1, 8, block), axis=0)
    weight = weight * scale
    x_re = x_re * weight
    x_im = x_im * weight
    coarse = depth // COARSE
    for m in range(templates):
        c0 = chirp_ref[m, 0, coarse:, :]
        s0 = chirp_ref[m, 1, coarse:, :]
        for i in range(coarse):
            span = slice(i * COARSE, (i + 1) * COARSE)
            c1 = chirp_ref[m, 0, i : i + 1, :]
            s1 = chirp_ref[m, 1, i : i + 1, :]
            c = c1 * c0 - s1 * s0
            s = s1 * c0 + c1 * s0
            a, b = x_re[span], x_im[span]
            re_ref[m, span, :] = a * c - b * s
            im_ref[m, span, :] = a * s + b * c


def inverse_kernel(
    block, templates,
    re_ref, im_ref, i1_ref, twist_ref, i2_ref, sigma_ref,
    out_ref,
    c_buf, i1_buf, i2_buf, g_buf,
):
    step = pl.program_id(0)
    inner = re_ref.shape[2]
    depth = re_ref.shape[1]
    half = i2_buf.shape[2]
    i1_coarse = i1_ref.shape[1] - FINE
    i2_coarse = i2_ref.shape[1] - FINE
    twist_coarse = twist_ref.shape[1] - FINE

    @pl.when(step == 0)
    def _():
        for m in range(templates):
            lanes = slice(m * inner, (m + 1) * inner)
            for first in range(0, depth, COARSE):
                rows = slice(first, first + COARSE)
                re = re_ref[m, rows, :]
                im = im_ref[m, rows, :]
                put(c_buf, 0, (rows, lanes), re + im)
                put(c_buf, 1, (rows, lanes), re)
                put(c_buf, 2, (rows, lanes), im)

        @pl.loop(0, i2_coarse)
        def _(outer):
            c, s = product_rows(i2_ref, outer, i2_coarse)
            put_factor(i2_buf, (pl.ds(pl.multiple_of(outer * FINE, FINE), FINE),), c, s)

    per_block = block // FINE

    @pl.loop(0, per_block)
    def _(i):
        rows = (pl.ds(pl.multiple_of(i * FINE, FINE), FINE),)
        c, s = product_rows(i1_ref, step * per_block + i, i1_coarse)
        put_factor(i1_buf, rows, c, s)

    total = jnp.sum(jnp.sum(sigma_ref[...], axis=0, keepdims=True), axis=1, keepdims=True)
    norm = 1.0 / jnp.sqrt(total)
    g_re, g_im = complex_dot(i1_buf, c_buf, NN)
    quarters = block // LANE
    row_stride = templates * (i1_coarse * FINE // LANE)
    for i in range(per_block):
        span = slice(i * FINE, (i + 1) * FINE)
        c, s = product_rows(twist_ref, step * per_block + i, twist_coarse)
        for m in range(templates):
            lanes = slice(m * inner, (m + 1) * inner)
            a, b = g_re[span, lanes], g_im[span, lanes]
            re = a * c - b * s
            im = a * s + b * c
            put(g_buf.at[m], 0, (span,), re + im)
            put(g_buf.at[m], 1, (span,), re)
            put(g_buf.at[m], 2, (span,), im)
    for m in range(templates):
        z_re, z_im = complex_dot(i2_buf, g_buf.at[m], NT)
        size = jnp.sqrt(z_re * z_re + z_im * z_im) * norm
        for q in range(quarters):
            first = (step * quarters + q) * templates + m
            out_ref[pl.ds(first, half, stride=row_stride), :] = size[:, q * LANE : (q + 1) * LANE]


def local(strain, psd_bins, psd_values, chirp_slope, chirp_curve):
    groups = lax.axis_size("tmpl")
    own_part = strain[0]
    half_len = own_part.shape[0]
    sub_len = 2 * half_len
    total_len = sub_len * groups
    inner = sub_len // LANE
    outer = total_len // inner
    depth = 3 * outer // 8
    k_low = total_len // 200
    k_cut = 3 * total_len // 8
    bands = 3 * groups // 8
    templates = chirp_slope.shape[0]
    member_len = psd_bins.shape[1]
    member_rows = member_len // inner
    assert (COARSE * inner) ** 2 % total_len == 0 and 2 * COARSE * inner**2 % total_len == 0
    assert total_len & (total_len - 1) == 0

    extra = bands * member_len // LANE
    table_shapes = [
        jax.ShapeDtypeStruct((templates, 2, depth // COARSE + COARSE, inner), F32),
        jax.ShapeDtypeStruct((depth, inner), F32),
    ]
    vmem = pl.BlockSpec(memory_space=pltpu.VMEM)
    smem = pl.BlockSpec(memory_space=pltpu.SMEM)
    own_rows = own_part.reshape(-1, LANE)
    rows = 2 * own_rows.shape[0] + extra
    if groups == 8:
        packed, chirp, amplitude = pl.pallas_call(
            functools.partial(gather_kernel, bands, inner, total_len),
            in_specs=[vmem, vmem, vmem, smem, smem],
            out_specs=[vmem, vmem, vmem],
            out_shape=[jax.ShapeDtypeStruct((groups, rows, LANE), F32)] + table_shapes,
            scratch_shapes=[
                pltpu.VMEM((extra, LANE), jnp.int32),
                pltpu.SemaphoreType.DMA((3, 9)),
                pltpu.SemaphoreType.DMA((3, 9)),
                pltpu.SemaphoreType.DMA((5,)),
                pltpu.SemaphoreType.DMA((5,)),
            ],
            compiler_params=pltpu.CompilerParams(collective_id=0, has_side_effects=True),
            name="gather",
        )(own_rows, psd_bins, psd_values, chirp_slope, chirp_curve)
    else:
        tail = shifted(own_part, "tm", 1).reshape(-1, LANE)
        inv_psd = pl.pallas_call(
            functools.partial(density_kernel, bands, inner),
            out_shape=jax.ShapeDtypeStruct((extra, LANE), F32),
            scratch_shapes=[pltpu.VMEM((extra, LANE), jnp.int32)],
            name="density",
        )(psd_bins, psd_values)
        packed = lax.all_gather(
            jnp.concatenate([tail, own_rows, inv_psd], axis=0), "tmpl", axis=0, tiled=False
        )
        chirp, amplitude = pl.pallas_call(
            functools.partial(table_kernel, total_len),
            in_specs=[smem, smem],
            out_shape=table_shapes,
            name="tables",
        )(chirp_slope, chirp_curve)

    place = np.arange(outer)
    sample = (place % LANE) * groups + place // LANE
    f1 = base_table(inner, np.arange(inner), inner, -1.0)
    twist1 = base_table(inner, sample, total_len, -1.0)
    f2 = base_table(depth, sample, outer, -1.0)
    i1 = base_table(outer, np.arange(depth), outer, 1.0)
    twist2 = base_table(outer, np.arange(inner), total_len, 1.0)
    i2 = base_table(inner // 2, np.arange(inner), inner, 1.0, inner // 2)

    block = 2 * LANE
    whole = lambda *shape: pl.BlockSpec(shape, lambda i: (0,) * len(shape))
    full = lambda array: whole(*array.shape)
    coef_re, coef_im, sigma = pl.pallas_call(
        functools.partial(
            forward_kernel, block, inner, member_rows, templates, 1.0 / math.sqrt(total_len)
        ),
        grid=(inner // block,),
        in_specs=[
            full(packed), full(f1), full(twist1), full(f2),
            pl.BlockSpec((depth, block), lambda i: (0, i)),
            pl.BlockSpec((templates, 2, chirp.shape[2], block), lambda i: (0, 0, 0, i)),
        ],
        out_specs=[
            pl.BlockSpec((templates, depth, block), lambda i: (0, 0, i)),
            pl.BlockSpec((templates, depth, block), lambda i: (0, 0, i)),
            whole(8, block),
        ],
        out_shape=[
            jax.ShapeDtypeStruct((templates, depth, inner), F32),
            jax.ShapeDtypeStruct((templates, depth, inner), F32),
            jax.ShapeDtypeStruct((8, block), F32),
        ],
        scratch_shapes=[
            pltpu.VMEM((2, inner, outer), BF16),
            pltpu.VMEM((2, 2, block, inner), BF16),
            pltpu.VMEM((3, 2, block, outer), BF16),
            pltpu.VMEM((3, 2, depth, outer), BF16),
            pltpu.VMEM((depth, block), F32),
        ],
        compiler_params=pltpu.CompilerParams(vmem_limit_bytes=VMEM_LIMIT),
        name="forward",
    )(packed, f1, twist1, f2, amplitude, chirp)

    half = inner // 2
    rows = half * (outer // LANE) * templates
    flat = pl.pallas_call(
        functools.partial(inverse_kernel, block, templates),
        grid=(outer // block,),
        in_specs=[
            full(coef_re), full(coef_im), full(i1), full(twist2), full(i2), full(sigma),
        ],
        out_specs=whole(rows, LANE),
        out_shape=jax.ShapeDtypeStruct((rows, LANE), F32),
        scratch_shapes=[
            pltpu.VMEM((3, 2, depth, templates * inner), BF16),
            pltpu.VMEM((3, 2, block, depth), BF16),
            pltpu.VMEM((3, 2, half, inner), BF16),
            pltpu.VMEM((templates, 3, 2, block, inner), BF16),
        ],
        compiler_params=pltpu.CompilerParams(vmem_limit_bytes=VMEM_LIMIT),
        name="inverse",
    )(coef_re, coef_im, i1, twist2, i2, sigma)
    result = flat.reshape(-1, templates, LANE)
    return jnp.transpose(result, (1, 0, 2)).reshape(templates, -1)


def solution(mesh):
    placed = (P("tmpl", "tm"), P(None, "tmpl"), P("tm", None), P("tmpl"), P("tmpl"))
    return jax.shard_map(
        local, mesh=mesh, in_specs=placed, out_specs=P("tmpl", "tm"), check_vma=False
    )
```

profile of v0, /device:TPU:0, one launch (start us, length us, event | category | flops | bytes accessed | tf_op | source)
XLA Modules:
  0.0 63.4 jit_solution(5648158335707790913)
XLA Ops:
  0.0 28.1 %gather.1 = (f32[8,704,128]{2,1,0:T(8,128)}, f32[2,2,40,512]{3,2,1,0:T(8,128)}, f32[384,512]{1,0:T(8,128)}) custom-call(f32[256,128]{1,0:T(8,128)} %bitcast.6, s32[4,8192]{1,0:T(4,128)} %bins_ref.1, f32[1,8192]{1,0:T(1,128)} %table_ref.1, s32[2]{0:T(128)} %slope_ref.1, s32[2]{0:T(128)} %curve_ref.1), custom_call_target="tpu_custom_call" | custom-call | tf_op jit(solution)/shard_map/gather/pallas_call | solution.py:531
  28.1 15.2 %forward.1 = (f32[2,384,512]{2,1,0:T(8,128)}, f32[2,384,512]{2,1,0:T(8,128)}, f32[8,256]{1,0:T(8,128)}) custom-call(f32[8,704,128]{2,1,0:T(8,128)} %get-tuple-element.11.packed_ref, f32[2,48,512]{2,1,0:T(8,128)} %constant.12.clone.f1_ref, f32[2,48,1024]{2,1,0:T(8,128)} %constant.13.clone.twist_ref, f32[2,44,1024]{2,1,0:T(8,128)} %constant.14.clone.f2_ref, ...), custom_call_target="tpu_custom_call" | custom-call | tf_op jit(solution)/shard_map/forward/pallas_call | solution.py:576
  43.3 20.1 %inverse.1 = f32[4096,128]{1,0:T(8,128)} custom-call(f32[2,384,512]{2,1,0:T(8,128)} %get-tuple-element.14.re_ref, f32[2,384,512]{2,1,0:T(8,128)} %get-tuple-element.15.im_ref, f32[2,64,384]{2,1,0:T(8,128)} %constant.15.clone.i1_ref, f32[2,64,512]{2,1,0:T(8,128)} %constant.16.clone.twist_ref, f32[2,40,512]{2,1,0:T(8,128)} %constant.17.clone.i2_ref, ...), custom_call_target="tpu_custom_call" | custom-call | tf_op jit(solution)/shard_map/inverse/pallas_call | solution.py:609
where the time goes:
time: 63.8 us; the launch traced here: 63.4 us
  Pallas kernels  63.4 us (99%)
    pallas_call x1, Pallas kernels, local(): pl.pallas_call(functools.partial(gather_kernel, bands, inner, total_len),...  28.1 us
    pallas_call x1, Pallas kernels, local(): pl.pallas_call(functools.partial(inverse_kernel, block, templates), grid=...  20.1 us
    pallas_call x1, Pallas kernels, local(): pl.pallas_call(functools.partial(forward_kernel, block, inner, member_row...  15.2 us

commit v1 on v0

v1 whole, which is shorter than its diff:
```python
import functools
import math

import jax
import jax.numpy as jnp
import numpy as np
from jax import lax
from jax.experimental import pallas as pl
from jax.experimental.pallas import tpu as pltpu
from jax.sharding import PartitionSpec as P

TWO_PI = 2.0 * math.pi
LANE = 128
FINE = 32
COARSE = 16
VMEM_LIMIT = 63 * 1024 * 1024
BF16 = jnp.bfloat16
F32 = jnp.float32
NN = (((1,), (0,)), ((), ()))
NT = (((1,), (1,)), ((), ()))


def shifted(block, axis, distance):
    devices = range(lax.axis_size(axis))
    route = [(i - distance, i) for i in devices if i - distance in devices]
    return lax.ppermute(block, axis, route)


def factor_table(coarse, fine, cols, modulus, direction):
    index = np.concatenate([np.asarray(coarse), np.asarray(fine)]).astype(np.int64)
    angle = (index[:, None] * np.asarray(cols, dtype=np.int64)[None, :] % modulus) * (
        direction * TWO_PI / modulus
    )
    return jnp.asarray(np.stack([np.cos(angle), np.sin(angle)]).astype(np.float32))


def base_table(rows, cols, modulus, direction):
    return factor_table(FINE * np.arange(rows // FINE), np.arange(FINE), cols, modulus, direction)


def product_rows(table, outer, lanes=slice(None), fine=FINE):
    coarse = table.shape[1] - fine
    c1 = table[0, pl.ds(outer, 1), :][:, lanes]
    s1 = table[1, pl.ds(outer, 1), :][:, lanes]
    c0 = table[0, coarse:, lanes]
    s0 = table[1, coarse:, lanes]
    return c1 * c0 - s1 * s0, s1 * c0 + c1 * s0


def halves(value):
    high = value.astype(BF16)
    return high, (value - high.astype(F32)).astype(BF16)


def put(ref, index, value):
    high, low = halves(value)
    ref[(0,) + index] = high
    ref[(1,) + index] = low


def put_turn(ref, first, rows, lane, lanes, height, width, c, s):
    for part, value in ((0, c), (1, s)):
        high, low = halves(value)
        for slot, piece in ((0, high), (1, low)):
            ref[slot, pl.ds(first + part * height, rows), lane : lane + lanes] = piece
            other = piece if part == 0 else -piece
            ref[slot, pl.ds(first + (1 - part) * height, rows), lane + width : lane + width + lanes] = other


def split_dot(a, b, dims):
    ((a_axis,), (b_axis,)), _ = dims
    left = jnp.concatenate([a[0], a[1], a[0]], axis=a_axis)
    right = jnp.concatenate([b[1], b[0], b[0]], axis=b_axis)
    return lax.dot_general(left, right, dims, preferred_element_type=F32)


def turn(value, numerator, count):
    re, im = value
    step = numerator % count
    if step == 0:
        return re, im
    if 4 * step == count:
        return -im, re
    if 2 * step == count:
        return -re, -im
    if 4 * step == 3 * count:
        return im, -re
    c = math.cos(TWO_PI * step / count)
    s = math.sin(TWO_PI * step / count)
    if 8 * step % count == 0:
        size = math.sqrt(0.5)
        if (c > 0) == (s > 0):
            pair = (re - im) * size, (re + im) * size
        else:
            pair = (re + im) * size, (im - re) * size
        return pair if c > 0 else (-pair[0], -pair[1])
    return re * c - im * s, re * s + im * c


def small_dft(values, direction, wanted):
    count = len(values)
    if count == 1:
        return {0: values[0]}
    half = count // 2
    result = {}
    for odd in (0, 1):
        inner_wanted = [w // 2 for w in wanted if w % 2 == odd]
        if not inner_wanted:
            continue
        folded = []
        for j in range(half):
            (a, b), (c, d) = values[j], values[j + half]
            if odd:
                folded.append(turn((a - c, b - d), direction * j, count))
            else:
                folded.append((a + c, b + d))
        for w, value in small_dft(folded, direction, inner_wanted).items():
            result[2 * w + odd] = value
    return result


def look_up(bins, table_ref):
    high = bins // LANE
    low = bins % LANE

    def body(row, total):
        lanes = pl.ds(pl.multiple_of(row * LANE, LANE), LANE)
        line = jnp.broadcast_to(table_ref[:, lanes], bins.shape)
        return jnp.where(
            high == row,
            jnp.take_along_axis(line, low, axis=1, mode="promise_in_bounds"),
            total,
        )

    picked = lax.fori_loop(
        0, table_ref.shape[1] // LANE, body, jnp.ones(bins.shape, F32), unroll=4
    )
    return 1.0 / picked


def density_rows(bins_ref, ordered_ref, bands, inner):
    member_rows = bins_ref.shape[1] // inner
    for q in range(inner // LANE):
        for band in range(bands):
            for row in range(member_rows):
                start = row * inner + q * LANE
                target = (q * bands + band) * member_rows + row
                ordered_ref[target : target + 1, :] = bins_ref[
                    band : band + 1, start : start + LANE
                ]


def density_kernel(bands, inner, bins_ref, table_ref, out_ref, ordered_ref):
    density_rows(bins_ref, ordered_ref, bands, inner)
    out_ref[...] = look_up(ordered_ref[...], table_ref)


def amplitude_rows(first, fold, reach, shape, total_len):
    k_low = total_len // 200
    k_cut = 3 * total_len // 8
    member = first // reach
    row = fold * (first - member * reach + lax.broadcasted_iota(jnp.int32, shape, 0)) + member
    frequency = row * shape[1] + lax.broadcasted_iota(jnp.int32, shape, 1)
    ratio = jnp.maximum(frequency.astype(F32) / k_low, 1.0)
    inside = (frequency >= k_low) & (frequency < k_cut)
    return jnp.where(inside, jnp.exp(jnp.log(ratio) * (-7.0 / 6.0)), 0.0)


def template_rows(slope_ref, curve_ref, chirp_ref, m, total_len):
    inner = chirp_ref.shape[3]
    fold = (chirp_ref.shape[2] - COARSE) // 8
    for first in range(0, COARSE + 8 * fold, 8):
        slope = slope_ref[m]
        curve = curve_ref[m]
        shape = (8, inner)
        row = lax.broadcasted_iota(jnp.int32, shape, 0)
        column = lax.broadcasted_iota(jnp.int32, shape, 1)
        mask = total_len - 1
        if first < COARSE:
            far = (8 * fold * inner) * (first + row)
            phase = slope * far + curve * ((2 * far * column) & mask)
        else:
            near = inner * (fold * row + (first - COARSE) // 8) + column
            phase = slope * near + curve * ((near * near) & mask)
        angle = (phase & mask).astype(F32) * (TWO_PI / total_len)
        chirp_ref[m, 0, first : first + 8, :] = jnp.cos(angle)
        chirp_ref[m, 1, first : first + 8, :] = jnp.sin(angle)


def amplitude_table(amp_ref, fold, total_len):
    depth, inner = amp_ref.shape
    reach = depth // fold

    @pl.loop(0, depth // 8)
    def _(i):
        first = pl.multiple_of(i * 8, 8)
        amp_ref[pl.ds(first, 8), :] = amplitude_rows(first, fold, reach, (8, inner), total_len)


def table_kernel(total_len, slope_ref, curve_ref, chirp_ref, amp_ref):
    for m in range(chirp_ref.shape[0]):
        template_rows(slope_ref, curve_ref, chirp_ref, m, total_len)
    amplitude_table(amp_ref, (chirp_ref.shape[2] - COARSE) // 8, total_len)


def gather_kernel(
    bands, inner, total_len,
    own_ref, bins_ref, table_ref, slope_ref, curve_ref,
    out_ref, chirp_ref, amp_ref,
    ordered_ref, send_sem, recv_sem, tail_send, tail_recv,
):
    tm = lax.axis_index("tm")
    me = lax.axis_index("tmpl")
    count = lax.axis_size("tm")
    half = own_ref.shape[0]
    extra = ordered_ref.shape[0]

    def peer(distance):
        low = me % (2 * distance)
        return me - low + (low + distance) % (2 * distance)

    core = peer(1)
    side = peer(2)
    front = peer(4)
    side_front = side + front - me
    spans = ((half, half), (0, half), (2 * half, extra))

    barrier = pltpu.get_barrier_semaphore()
    for other in (core, side, front):
        pl.semaphore_signal(
            barrier, inc=1, device_id={"tmpl": other}, device_id_type=pl.DeviceIdType.MESH
        )

    for other in ((tm + 1) % count, (tm + count - 1) % count):
        pl.semaphore_signal(
            barrier, inc=1, device_id={"tm": other}, device_id_type=pl.DeviceIdType.MESH
        )
    pl.semaphore_wait(barrier, 5)

    def copy(part, kind, slot, piece, target, source=None):
        first, rows = spans[part]
        if part == 1 and kind in (1, 2):
            piece = 2 - kind
        if piece is not None:
            rows = rows // 2
            first = first + piece * rows
        view = out_ref.at[slot, pl.ds(first, rows), :]
        return pltpu.make_async_remote_copy(
            src_ref=view if source is None else source,
            dst_ref=view,
            send_sem=send_sem.at[part, kind],
            recv_sem=recv_sem.at[part, kind],
            device_id={"tmpl": target},
            device_id_type=pl.DeviceIdType.MESH,
        )

    def send(part, kind, source=None):
        slot, piece, target = (
            (me, None, core), (me, None, side), (me, None, front),
            (side, None, core), (front, None, core),
            (side, 0, front), (front, 1, side),
            (side_front, 0, core), (side_front, 1, core),
        )[kind]
        return copy(part, kind, slot, piece, target, source if kind < 3 else None)

    def first_stage(part, source=None):
        send(part, 1, source).start()
        send(part, 2, source).start()
        send(part, 0, source).start()

    def second_stage(part):
        copy(part, 1, side, None, side).wait_recv()
        send(part, 5).start()
        copy(part, 2, front, None, front).wait_recv()
        send(part, 6).start()
        send(part, 3).start()
        send(part, 4).start()

    def third_stage(part):
        copy(part, 5, side_front, 0, front).wait_recv()
        send(part, 7).start()
        copy(part, 6, side_front, 1, side).wait_recv()
        send(part, 8).start()

    def last_stage(part, source=None):
        other = core + side - me
        across = core + front - me
        corner = core + side_front - me
        copy(part, 0, core, None, core).wait_recv()
        copy(part, 3, other, None, core).wait_recv()
        copy(part, 4, across, None, core).wait_recv()
        copy(part, 7, corner, 0, core).wait_recv()
        copy(part, 8, corner, 1, core).wait_recv()
        for kind in range(9):
            if part != 1 or kind not in (5, 6):
                send(part, kind, source).wait_send()

    def onward(kind):
        slot, piece = ((me, None), (side, 0), (front, 1), (side_front, 0), (side_front, 1))[kind]
        rows = half if piece is None else half // 2
        first = 0 if piece is None else piece * rows
        source = own_ref if kind == 0 else out_ref.at[slot, pl.ds(half + first, rows), :]
        return pltpu.make_async_remote_copy(
            src_ref=source,
            dst_ref=out_ref.at[slot, pl.ds(first, rows), :],
            send_sem=tail_send.at[kind],
            recv_sem=tail_recv.at[kind],
            device_id={"tm": (tm + 1) % count},
            device_id_type=pl.DeviceIdType.MESH,
        )

    def pass_on(kinds):
        @pl.when(tm < count - 1)
        def _():
            for kind in kinds:
                onward(kind).start()

    def second_stage_old():
        copy(1, 1, side, None, side).wait_recv()
        onward(1).wait_recv()
        send(1, 3).start()
        copy(1, 2, front, None, front).wait_recv()
        onward(2).wait_recv()
        send(1, 4).start()

    def third_stage_old():
        onward(3).wait_recv()
        send(1, 7).start()
        onward(4).wait_recv()
        send(1, 8).start()

    pass_on((0,))
    first_stage(0, own_ref)
    out_ref[me, half : 2 * half, :] = own_ref[...]
    density_rows(bins_ref, ordered_ref, bands, inner)
    third = extra // 3

    def densities(i):
        rows = slice(i * third, (i + 1) * third)
        out_ref[me, 2 * half + i * third : 2 * half + (i + 1) * third, :] = look_up(
            ordered_ref[rows, :], table_ref
        )

    @pl.when(tm == 0)
    def _():
        for slot in range(out_ref.shape[0]):
            out_ref[slot, :half, :] = jnp.zeros((half, LANE), F32)

    @pl.when(tm > 0)
    def _():
        onward(0).wait_recv()
        first_stage(1)

    densities(0)
    second_stage(0)
    pass_on((1, 2))
    densities(1)
    third_stage(0)
    pass_on((3, 4))
    densities(2)
    first_stage(2)

    @pl.when(tm > 0)
    def _():
        second_stage_old()

    template_rows(slope_ref, curve_ref, chirp_ref, 0, total_len)
    second_stage(2)

    @pl.when(tm > 0)
    def _():
        third_stage_old()

    for m in range(1, chirp_ref.shape[0]):
        template_rows(slope_ref, curve_ref, chirp_ref, m, total_len)
    third_stage(2)
    amplitude_table(amp_ref, (chirp_ref.shape[2] - COARSE) // 8, total_len)
    last_stage(0, own_ref)

    @pl.when(tm > 0)
    def _():
        last_stage(1)

    last_stage(2)

    @pl.when(tm < count - 1)
    def _():
        for kind in range(5):
            onward(kind).wait_send()


def filter_kernel(
    segment_rows, member_rows, bands, templates, scale,
    packed_ref, amp_ref, chirp_ref, f1_ref, twist1_ref, f2_ref, i1_ref, twist2_ref, i2_ref,
    out_ref,
    f1_buf, x_buf, f2_buf, y_buf, part_ref, weight_ref, c_buf, i1_buf, i2_buf, g_buf,
):
    groups = packed_ref.shape[0]
    inner = amp_ref.shape[1]
    half = inner // 2
    fold = c_buf.shape[1]
    reach = amp_ref.shape[0] // fold
    band_rows = LANE // fold

    for a in range(2):
        for outer in range(half // FINE):
            for lane in range(0, half, LANE):
                c, s = product_rows(f1_ref, outer, slice(a * half + lane, a * half + lane + LANE))
                put(f1_buf.at[a], (slice(outer * FINE, (outer + 1) * FINE), slice(lane, lane + LANE)), c)
                put(
                    f1_buf.at[a],
                    (slice(half + outer * FINE, half + (outer + 1) * FINE), slice(lane, lane + LANE)),
                    s,
                )
    for j in range(groups):
        for a in range(fold):
            c, s = product_rows(f2_ref, a, slice(j * LANE, (j + 1) * LANE), band_rows)
            put_turn(f2_buf.at[j], a * band_rows, band_rows, 0, LANE, LANE, LANE, c, s)

    for pair in range(groups // 2):
        for a in range(2):
            for side in range(2):
                j = 2 * pair + side
                for first in range(0, half, FINE):
                    value = packed_ref[j, pl.ds(2 * first + a, FINE, stride=2), :]
                    put(
                        x_buf.at[pair % x_buf.shape[0], a],
                        (slice(first, first + FINE), slice(side * LANE, (side + 1) * LANE)),
                        value,
                    )
        even = split_dot(f1_buf.at[0], x_buf.at[pair % x_buf.shape[0], 0], NN)
        odd = split_dot(f1_buf.at[1], x_buf.at[pair % x_buf.shape[0], 1], NN)
        for block in range(half // FINE):
            rows = slice(block * FINE, (block + 1) * FINE)
            lower = slice(half + block * FINE, half + (block + 1) * FINE)
            for side in range(2):
                j = 2 * pair + side
                lanes = slice(side * LANE, (side + 1) * LANE)
                for r in range(2):
                    c, s = product_rows(
                        twist1_ref, r * (half // FINE) + block, slice(j * LANE, (j + 1) * LANE)
                    )
                    if r:
                        a, b = even[rows, lanes] - odd[rows, lanes], even[lower, lanes] - odd[lower, lanes]
                    else:
                        a, b = even[rows, lanes] + odd[rows, lanes], even[lower, lanes] + odd[lower, lanes]
                    target = slice(r * half + block * FINE, r * half + (block + 1) * FINE)
                    put(y_buf.at[j % y_buf.shape[0]], (target, slice(0, LANE)), a * c - b * s)
                    put(y_buf.at[j % y_buf.shape[0]], (target, slice(LANE, 2 * LANE)), a * s + b * c)
        for side in range(2):
            j = 2 * pair + side
            part_ref[j] = split_dot(f2_buf.at[j], y_buf.at[j % y_buf.shape[0]], NT)

    for q in range(inner // LANE):
        for band in range(bands):
            for j in range(groups):
                source = segment_rows + (q * bands + band) * member_rows
                target = (band * groups + j) * member_rows
                weight_ref[q, target : target + member_rows, :] = packed_ref[
                    j, source : source + member_rows, :
                ]

    for a in range(fold):
        @pl.loop(0, 1)
        def _(_):
            zero = jnp.zeros((LANE - reach, inner), BF16)
            for m in range(templates):
                for slot in range(2):
                    c_buf[m, a, slot, reach:LANE, :] = zero
                    c_buf[m, a, slot, LANE + reach :, :] = zero

    total = jnp.zeros((8, LANE), F32)
    for a in range(fold):
        for q0 in range(0, band_rows, COARSE):
            rows = slice(a * band_rows + q0, a * band_rows + q0 + COARSE)
            lower = slice(LANE + a * band_rows + q0, LANE + a * band_rows + q0 + COARSE)
            for lane in range(0, inner, LANE):
                lanes = slice(lane, lane + LANE)
                values = [
                    (part_ref[j, rows, lanes], part_ref[j, lower, lanes]) for j in range(groups)
                ]
                sums = small_dft(values, -1, list(range(bands)))
                for band in range(bands):
                    b = band * band_rows + q0
                    amp = amp_ref[a * reach + b : a * reach + b + COARSE, lanes]
                    density = weight_ref[lane // LANE, pl.ds(a + fold * b, COARSE, stride=fold), :]
                    weight = amp * density
                    power = weight * amp
                    total = total + power[:8] + power[8:]
                    weight = weight * scale
                    x_re = sums[band][0] * weight
                    x_im = sums[band][1] * weight
                    for m in range(templates):
                        cs, ss = [], []
                        for n in range(b // 8, b // 8 + COARSE // 8):
                            c1 = chirp_ref[m, 0, n : n + 1, lanes]
                            s1 = chirp_ref[m, 1, n : n + 1, lanes]
                            near = slice(COARSE + 8 * a, COARSE + 8 * (a + 1))
                            c0 = chirp_ref[m, 0, near, lanes]
                            s0 = chirp_ref[m, 1, near, lanes]
                            cs.append(c1 * c0 - s1 * s0)
                            ss.append(s1 * c0 + c1 * s0)
                        c = jnp.concatenate(cs, axis=0)
                        s = jnp.concatenate(ss, axis=0)
                        put(c_buf.at[m, a], (slice(b, b + COARSE), lanes), x_re * c - x_im * s)
                        put(
                            c_buf.at[m, a],
                            (slice(LANE + b, LANE + b + COARSE), lanes),
                            x_re * s + x_im * c,
                        )
    total = jnp.sum(jnp.sum(total, axis=0, keepdims=True), axis=1, keepdims=True)
    norm = 1.0 / jnp.sqrt(total)

    height = i2_buf.shape[2] // 2
    steps = half // LANE
    for rho in range(2):
        for outer in range(height // FINE):
            c, s = product_rows(i2_ref, rho * (height // FINE) + outer)
            put_turn(i2_buf.at[rho], outer * FINE, FINE, 0, half, height, half, c, s)

    per_step = LANE // FINE
    row_stride = 2 * templates * fold * steps

    @pl.loop(0, steps)
    def _(h):
        for a in range(fold):
            for o in range(per_step):
                c, s = product_rows(i1_ref, h * per_step + o, slice(a * LANE, (a + 1) * LANE))
                put_turn(i1_buf.at[a], o * FINE, FINE, 0, LANE, LANE, LANE, c, s)
        for m in range(templates):
            mixed = [split_dot(i1_buf.at[a], c_buf.at[m, a], NN) for a in range(fold)]
            for o in range(per_step):
                rows = slice(o * FINE, (o + 1) * FINE)
                lower = slice(LANE + o * FINE, LANE + (o + 1) * FINE)
                for lane in range(0, half, LANE):
                    sides = []
                    for first in (lane, half + lane):
                        lanes = slice(first, first + LANE)
                        values = [(mixed[a][rows, lanes], mixed[a][lower, lanes]) for a in range(fold)]
                        outs = small_dft(values, 1, list(range(fold)))
                        turned = []
                        for r in range(fold):
                            c, s = product_rows(
                                twist2_ref, (r * steps + h) * per_step + o, lanes
                            )
                            a, b = outs[r]
                            turned.append((a * c - b * s, a * s + b * c))
                        sides.append(turned)
                    for r in range(fold):
                        target = slice(r * LANE + o * FINE, r * LANE + (o + 1) * FINE)
                        for part in range(2):
                            near, far = sides[0][r][part], sides[1][r][part]
                            lanes = slice(part * half + lane, part * half + lane + LANE)
                            put(g_buf.at[m, 0], (target, lanes), near + far)
                            put(g_buf.at[m, 1], (target, lanes), near - far)
            for rho in range(2):
                z = split_dot(i2_buf.at[rho], g_buf.at[m, rho], NT)
                z_re, z_im = z[:height], z[height:]
                size = jnp.sqrt(z_re * z_re + z_im * z_im) * norm
                for r in range(fold):
                    first = ((rho * fold + r) * steps + h) * templates + m
                    out_ref[pl.ds(first, height, stride=row_stride), :] = size[:, r * LANE : (r + 1) * LANE]


def local(strain, psd_bins, psd_values, chirp_slope, chirp_curve):
    groups = lax.axis_size("tmpl")
    own_part = strain[0]
    half_len = own_part.shape[0]
    sub_len = 2 * half_len
    total_len = sub_len * groups
    inner = sub_len // LANE
    outer = total_len // inner
    depth = 3 * outer // 8
    k_low = total_len // 200
    k_cut = 3 * total_len // 8
    bands = 3 * groups // 8
    templates = chirp_slope.shape[0]
    member_len = psd_bins.shape[1]
    member_rows = member_len // inner
    fold = outer // (2 * LANE)
    reach = depth // fold
    assert (fold * inner) ** 2 % total_len == 0 and 2 * fold * inner**2 % total_len == 0
    assert total_len & (total_len - 1) == 0 and reach <= 8 * COARSE and reach <= LANE

    extra = bands * member_len // LANE
    table_shapes = [
        jax.ShapeDtypeStruct((templates, 2, COARSE + 8 * fold, inner), F32),
        jax.ShapeDtypeStruct((depth, inner), F32),
    ]
    vmem = pl.BlockSpec(memory_space=pltpu.VMEM)
    smem = pl.BlockSpec(memory_space=pltpu.SMEM)
    own_rows = own_part.reshape(-1, LANE)
    rows = 2 * own_rows.shape[0] + extra
    if groups == 8:
        packed, chirp, amplitude = pl.pallas_call(
            functools.partial(gather_kernel, bands, inner, total_len),
            in_specs=[vmem, vmem, vmem, smem, smem],
            out_specs=[vmem, vmem, vmem],
            out_shape=[jax.ShapeDtypeStruct((groups, rows, LANE), F32)] + table_shapes,
            scratch_shapes=[
                pltpu.VMEM((extra, LANE), jnp.int32),
                pltpu.SemaphoreType.DMA((3, 9)),
                pltpu.SemaphoreType.DMA((3, 9)),
                pltpu.SemaphoreType.DMA((5,)),
                pltpu.SemaphoreType.DMA((5,)),
            ],
            compiler_params=pltpu.CompilerParams(collective_id=0, has_side_effects=True),
            name="gather",
        )(own_rows, psd_bins, psd_values, chirp_slope, chirp_curve)
    else:
        tail = shifted(own_part, "tm", 1).reshape(-1, LANE)
        inv_psd = pl.pallas_call(
            functools.partial(density_kernel, bands, inner),
            out_shape=jax.ShapeDtypeStruct((extra, LANE), F32),
            scratch_shapes=[pltpu.VMEM((extra, LANE), jnp.int32)],
            name="density",
        )(psd_bins, psd_values)
        packed = lax.all_gather(
            jnp.concatenate([tail, own_rows, inv_psd], axis=0), "tmpl", axis=0, tiled=False
        )
        chirp, amplitude = pl.pallas_call(
            functools.partial(table_kernel, total_len),
            in_specs=[smem, smem],
            out_shape=table_shapes,
            name="tables",
        )(chirp_slope, chirp_curve)

    half = inner // 2
    place = np.arange(outer)
    sample = (place % LANE) * groups + place // LANE
    step = np.arange(half)
    band_rows = LANE // fold
    f1 = base_table(half, np.concatenate([2 * step, 2 * step + 1]), inner, -1.0)
    twist1 = base_table(inner, sample, total_len, -1.0)
    f2 = factor_table(np.arange(fold), fold * np.arange(band_rows), sample, outer, -1.0)
    member = np.arange(fold)[:, None] + fold * np.arange(LANE)[None, :]
    i1 = base_table(2 * LANE, member.reshape(-1), outer, 1.0)
    twist2 = base_table(outer, np.arange(inner), total_len, 1.0)
    late = half + np.arange(2)[:, None] + 2 * FINE * np.arange(half // 2 // FINE)[None, :]
    i2 = factor_table(late.reshape(-1), 2 * np.arange(FINE), step, inner, 1.0)

    out_rows = half * (outer // LANE) * templates
    flat = pl.pallas_call(
        functools.partial(
            filter_kernel, inner, member_rows, bands, templates, 1.0 / math.sqrt(total_len)
        ),
        in_specs=[vmem] * 9,
        out_specs=vmem,
        out_shape=jax.ShapeDtypeStruct((out_rows, LANE), F32),
        scratch_shapes=[
            pltpu.VMEM((2, 2, inner, half), BF16),
            pltpu.VMEM((2, 2, 2, half, 2 * LANE), BF16),
            pltpu.VMEM((groups, 2, 2 * LANE, 2 * LANE), BF16),
            pltpu.VMEM((4, 2, inner, 2 * LANE), BF16),
            pltpu.VMEM((groups, 2 * LANE, inner), F32),
            pltpu.VMEM((inner // LANE, depth, LANE), F32),
            pltpu.VMEM((templates, fold, 2, 2 * LANE, inner), BF16),
            pltpu.VMEM((fold, 2, 2 * LANE, 2 * LANE), BF16),
            pltpu.VMEM((2, 2, half, inner), BF16),
            pltpu.VMEM((templates, 2, 2, fold * LANE, inner), BF16),
        ],
        compiler_params=pltpu.CompilerParams(vmem_limit_bytes=VMEM_LIMIT),
        name="filter",
    )(packed, amplitude, chirp, f1, twist1, f2, i1, twist2, i2)
    result = flat.reshape(-1, templates, LANE)
    return jnp.transpose(result, (1, 0, 2)).reshape(templates, -1)


def solution(mesh):
    placed = (P("tmpl", "tm"), P(None, "tmpl"), P("tm", None), P("tmpl"), P("tmpl"))
    return jax.shard_map(
        local, mesh=mesh, in_specs=placed, out_specs=P("tmpl", "tm"), check_vma=False
    )
```

time: 63.8 us -> 52.3 us (0.82)
  Pallas kernels: 63.4 us -> 52.1 us
    pallas_call x2 -> x1, Pallas kernels: 35.3 us -> 23.7 us  [local(): pl.pallas_call(functools.partial(filter_kernel, inner, member_rows, bands...]
where the time goes in v1:
time: 52.3 us; the launch traced here: 52.1 us
  Pallas kernels  52.1 us (100%)
    pallas_call x1, Pallas kernels, local(): pl.pallas_call(functools.partial(gather_kernel, bands, inner, total_len),...  28.4 us
    pallas_call x1, Pallas kernels, local(): pl.pallas_call(functools.partial(filter_kernel, inner, member_rows, bands...  23.7 us

profile of v1, /device:TPU:0, one launch (start us, length us, event | category | flops | bytes accessed | tf_op | source)
XLA Modules:
  0.0 52.1 jit_solution(653350306015408521)
XLA Ops:
  0.0 28.4 %gather.1 = (f32[8,704,128]{2,1,0:T(8,128)}, f32[2,2,48,512]{3,2,1,0:T(8,128)}, f32[384,512]{1,0:T(8,128)}) custom-call(f32[256,128]{1,0:T(8,128)} %bitcast.6, s32[4,8192]{1,0:T(4,128)} %bins_ref.1, f32[1,8192]{1,0:T(1,128)} %table_ref.1, s32[2]{0:T(128)} %slope_ref.1, s32[2]{0:T(128)} %curve_ref.1), custom_call_target="tpu_custom_call" | custom-call | tf_op jit(solution)/shard_map/gather/pallas_call | solution.py:595
  28.4 23.7 %filter.1 = f32[4096,128]{1,0:T(8,128)} custom-call(f32[8,704,128]{2,1,0:T(8,128)} %get-tuple-element.8.packed_ref, f32[384,512]{1,0:T(8,128)} %get-tuple-element.9.amp_ref, f32[2,2,48,512]{3,2,1,0:T(8,128)} %get-tuple-element.10.chirp_ref, f32[2,40,512]{2,1,0:T(8,128)} %constant.12.clone.f1_ref, f32[2,48,1024]{2,1,0:T(8,128)} %constant.13.clone.twist1_ref, ...), custom_call_target="tpu_custom_call" | custom-call | tf_op jit(solution)/shard_map/filter/pallas_call | solution.py:643

commit v2 on v1

--- a/solution.py
+++ b/solution.py
@@ -333,48 +333,38 @@
     first_stage(0, own_ref)
     out_ref[me, half : 2 * half, :] = own_ref[...]
     density_rows(bins_ref, ordered_ref, bands, inner)
-    third = extra // 3
-
-    def densities(i):
-        rows = slice(i * third, (i + 1) * third)
-        out_ref[me, 2 * half + i * third : 2 * half + (i + 1) * third, :] = look_up(
-            ordered_ref[rows, :], table_ref
-        )
+    out_ref[me, 2 * half : 2 * half + extra, :] = look_up(ordered_ref[...], table_ref)
+    first_stage(2)
+    fold = (chirp_ref.shape[2] - COARSE) // 8
 
     @pl.when(tm == 0)
     def _():
         for slot in range(out_ref.shape[0]):
             out_ref[slot, :half, :] = jnp.zeros((half, LANE), F32)
 
+    template_rows(slope_ref, curve_ref, chirp_ref, 0, total_len)
     @pl.when(tm > 0)
     def _():
         onward(0).wait_recv()
         first_stage(1)
 
-    densities(0)
     second_stage(0)
     pass_on((1, 2))
-    densities(1)
     third_stage(0)
     pass_on((3, 4))
-    densities(2)
-    first_stage(2)
-
+    second_stage(2)
+    for m in range(1, chirp_ref.shape[0]):
+        template_rows(slope_ref, curve_ref, chirp_ref, m, total_len)
+    third_stage(2)
     @pl.when(tm > 0)
     def _():
         second_stage_old()
 
-    template_rows(slope_ref, curve_ref, chirp_ref, 0, total_len)
-    second_stage(2)
-
     @pl.when(tm > 0)
     def _():
         third_stage_old()
 
-    for m in range(1, chirp_ref.shape[0]):
-        template_rows(slope_ref, curve_ref, chirp_ref, m, total_len)
-    third_stage(2)
-    amplitude_table(amp_ref, (chirp_ref.shape[2] - COARSE) // 8, total_len)
+    amplitude_table(amp_ref, fold, total_len)
     last_stage(0, own_ref)
 
     @pl.when(tm > 0)
@@ -527,32 +517,41 @@
             for o in range(per_step):
                 c, s = product_rows(i1_ref, h * per_step + o, slice(a * LANE, (a + 1) * LANE))
                 put_turn(i1_buf.at[a], o * FINE, FINE, 0, LANE, LANE, LANE, c, s)
-        for m in range(templates):
-            mixed = [split_dot(i1_buf.at[a], c_buf.at[m, a], NN) for a in range(fold)]
-            for o in range(per_step):
-                rows = slice(o * FINE, (o + 1) * FINE)
-                lower = slice(LANE + o * FINE, LANE + (o + 1) * FINE)
-                for lane in range(0, half, LANE):
-                    sides = []
-                    for first in (lane, half + lane):
-                        lanes = slice(first, first + LANE)
-                        values = [(mixed[a][rows, lanes], mixed[a][lower, lanes]) for a in range(fold)]
+        mixed = [
+            [split_dot(i1_buf.at[a], c_buf.at[m, a], NN) for a in range(fold)]
+            for m in range(templates)
+        ]
+        for o in range(per_step):
+            rows = slice(o * FINE, (o + 1) * FINE)
+            lower = slice(LANE + o * FINE, LANE + (o + 1) * FINE)
+            for lane in range(0, half, LANE):
+                sides = []
+                for first in (lane, half + lane):
+                    lanes = slice(first, first + LANE)
+                    turns = [
+                        product_rows(twist2_ref, (r * steps + h) * per_step + o, lanes)
+                        for r in range(fold)
+                    ]
+                    both = []
+                    for m in range(templates):
+                        values = [(mixed[m][a][rows, lanes], mixed[m][a][lower, lanes]) for a in range(fold)]
                         outs = small_dft(values, 1, list(range(fold)))
-                        turned = []
-                        for r in range(fold):
-                            c, s = product_rows(
-                                twist2_ref, (r * steps + h) * per_step + o, lanes
-                            )
-                            a, b = outs[r]
-                            turned.append((a * c - b * s, a * s + b * c))
-                        sides.append(turned)
+                        both.append(
+                            [
+                                (a * c - b * s, a * s + b * c)
+                                for (a, b), (c, s) in ((outs[r], turns[r]) for r in range(fold))
+                            ]
+                        )
+                    sides.append(both)
+                for m in range(templates):
                     for r in range(fold):
                         target = slice(r * LANE + o * FINE, r * LANE + (o + 1) * FINE)
                         for part in range(2):
-                            near, far = sides[0][r][part], sides[1][r][part]
+                            near, far = sides[0][m][r][part], sides[1][m][r][part]
                             lanes = slice(part * half + lane, part * half + lane + LANE)
                             put(g_buf.at[m, 0], (target, lanes), near + far)
                             put(g_buf.at[m, 1], (target, lanes), near - far)
+        for m in range(templates):
             for rho in range(2):
                 z = split_dot(i2_buf.at[rho], g_buf.at[m, rho], NT)
                 z_re, z_im = z[:height], z[height:]

time: 52.3 us -> 47.5 us (0.908)
  Pallas kernels: 52.1 us -> 47.4 us
    pallas_call x1, Pallas kernels: 28.4 us -> 24.7 us  [local(): pl.pallas_call(functools.partial(gather_kernel, bands, inner, total_len),...]
    pallas_call x1, Pallas kernels: 23.7 us -> 22.7 us  [local(): pl.pallas_call(functools.partial(filter_kernel, inner, member_rows, bands...]
where the time goes in v2:
time: 47.5 us; the launch traced here: 47.4 us
  Pallas kernels  47.4 us (100%)
    pallas_call x1, Pallas kernels, local(): pl.pallas_call(functools.partial(gather_kernel, bands, inner, total_len),...  24.7 us
    pallas_call x1, Pallas kernels, local(): pl.pallas_call(functools.partial(filter_kernel, inner, member_rows, bands...  22.7 us

profile of v2, /device:TPU:0, one launch (start us, length us, event | category | flops | bytes accessed | tf_op | source)
XLA Modules:
  0.0 47.4 jit_solution(13905362572317569112)
XLA Ops:
  0.0 24.7 %gather.1 = (f32[8,704,128]{2,1,0:T(8,128)}, f32[2,2,48,512]{3,2,1,0:T(8,128)}, f32[384,512]{1,0:T(8,128)}) custom-call(f32[256,128]{1,0:T(8,128)} %bitcast.6, s32[4,8192]{1,0:T(4,128)} %bins_ref.1, f32[1,8192]{1,0:T(1,128)} %table_ref.1, s32[2]{0:T(128)} %slope_ref.1, s32[2]{0:T(128)} %curve_ref.1), custom_call_target="tpu_custom_call" | custom-call | tf_op jit(solution)/shard_map/gather/pallas_call | solution.py:594
  24.7 22.7 %filter.1 = f32[4096,128]{1,0:T(8,128)} custom-call(f32[8,704,128]{2,1,0:T(8,128)} %get-tuple-element.8.packed_ref, f32[384,512]{1,0:T(8,128)} %get-tuple-element.9.amp_ref, f32[2,2,48,512]{3,2,1,0:T(8,128)} %get-tuple-element.10.chirp_ref, f32[2,40,512]{2,1,0:T(8,128)} %constant.12.clone.f1_ref, f32[2,48,1024]{2,1,0:T(8,128)} %constant.13.clone.twist1_ref, ...), custom_call_target="tpu_custom_call" | custom-call | tf_op jit(solution)/shard_map/filter/pallas_call | solution.py:642
